TPU v7x, 32 devices: a whole 2x2x4 slice. The times are simulated.
32 devices in a mesh: dp: 8 (over z, x), ctx: 4 (over y, core).
Axes of the slice: x: 2, y: 2, z: 4, core: 2. Of those that a mesh axis runs over, the one named last changes fastest.
Arguments:
- tokens: bfloat16 [16, 1024, 960], P('dp', 'ctx'), may hold values from -6 to 6
- segment_ids: int32 [16, 1024], P('dp', 'ctx'), may hold values from 0 to 5, as said below
- positions: int32 [16, 1024], P('dp', 'ctx'), may hold values from 0 to 2047, as said below
- norm_attn: float32 [960], replicated, may hold values from 0.25 to 1.75
- w_query: bfloat16 [921600], P(('dp', 'ctx')), may hold values from -0.1875 to 0.1875
- w_key: bfloat16 [307200], P(('dp', 'ctx')), may hold values from -0.1875 to 0.1875
- w_value: bfloat16 [307200], P(('dp', 'ctx')), may hold values from -0.1875 to 0.1875
- w_out: bfloat16 [921600], P(('dp', 'ctx')), may hold values from -0.75 to 0.75
- norm_ffn: float32 [960], replicated, may hold values from 0.25 to 1.75
- w_gate: bfloat16 [2457600], P(('dp', 'ctx')), may hold values from -0.1875 to 0.1875
- w_up: bfloat16 [2457600], P(('dp', 'ctx')), may hold values from -0.1875 to 0.1875
- w_down: bfloat16 [2457600], P(('dp', 'ctx')), may hold values from -0.125 to 0.125
- cotangent: bfloat16 [16, 1024, 960], P('dp', 'ctx'), may hold values from -6 to 6
Outputs:
- output: bfloat16 [16, 1024, 960], P('dp', 'ctx')
- d_tokens: float32 [16, 1024, 960], P('dp', 'ctx')
- d_norm_attn: float32 [960], replicated
- d_w_query: float32 [921600], P(('dp', 'ctx'))
- d_w_key: float32 [307200], P(('dp', 'ctx'))
- d_w_value: float32 [307200], P(('dp', 'ctx'))
- d_w_out: float32 [921600], P(('dp', 'ctx'))
- d_norm_ffn: float32 [960], replicated
- d_w_gate: float32 [2457600], P(('dp', 'ctx'))
- d_w_up: float32 [2457600], P(('dp', 'ctx'))
- d_w_down: float32 [2457600], P(('dp', 'ctx'))
Inputs may be any that keep to these rules, and one draw needn't show every extreme that they name: `segment_ids`: within each sequence the ids start at 0 and never fall. A run of one id is one document: a sequence's first run may be the rest of a longer document and has 102 positions or more, every later run is a document of 204 to 2047 positions, cut at the sequence's end. Within each run of one segment id the positions rise by one from token to token; every run but a sequence's first starts at 0, a sequence's first run starts at most at 1024.
All inputs are finite; a program needn't handle non-finite values.
Results may differ from a plain program's by a relative error of at most 0.02.
Values may be sent and summed in bfloat16 or wider, within the bound.
No kernel may reach another device: no remote copies, remote signals or barrier semaphores. Data moves between devices by JAX's collectives and lax.ppermute only.
A program may use at most 448 MiB of HBM per device.

v0:
```python
import jax
import jax.numpy as jnp
from jax import lax
from jax.sharding import PartitionSpec as P

D = 960
HEADS = 15
KV_HEADS = 5
HEAD_DIM = 64
FF = 2560
MICRO = 2
norm_eps = 1e-05
rope_base = 100000.0
mask_fill = -1000000000.0


def rms_scale(values):
    return lax.rsqrt(jnp.mean(values * values, axis=-1, keepdims=True) + norm_eps)


def norm_back(values, scale, gain, grad):
    gain_grad = jnp.sum(grad * values * scale, axis=0)
    weighted = grad * gain
    inner = jnp.mean(weighted * values, axis=-1, keepdims=True)
    return (scale * weighted - values * (scale * scale * scale) * inner, gain_grad)


def rope_tables(position):
    freqs = rope_base ** (-jnp.arange(0, HEAD_DIM, 2, dtype=jnp.float32) / HEAD_DIM)
    angles = position.astype(jnp.float32)[..., None] * freqs
    angles = jnp.concatenate([angles, angles], axis=-1)
    return (jnp.cos(angles)[..., None, :], jnp.sin(angles)[..., None, :])


def rotate(values, cosine, sine):
    half = values.shape[-1] // 2
    turned = jnp.concatenate([-values[..., half:], values[..., :half]], axis=-1)
    return values * cosine + turned * sine


def rotate_back(grad, cosine, sine):
    half = grad.shape[-1] // 2
    scaled = grad * sine
    return grad * cosine + jnp.concatenate([scaled[..., half:], -scaled[..., :half]], axis=-1)


def product(left, right):
    return jnp.dot(left, right, preferred_element_type=jnp.float32)


def product_left(left, right):
    return lax.dot_general(
        left, right, (((0,), (0,)), ((), ())), preferred_element_type=jnp.float32
    )


def product_right(left, right):
    return lax.dot_general(
        left, right, (((1,), (1,)), ((), ())), preferred_element_type=jnp.float32
    )


def masked_scores(query_groups, key_heads, allowed, score_scale):
    scores = (
        jnp.einsum("sckgd,slkd->skgcl", query_groups, key_heads, preferred_element_type=jnp.float32)
        * score_scale
    )
    return jnp.where(allowed, scores, mask_fill)


def owner_blocks(terms):
    dp_size = lax.axis_size("dp")
    ctx_size = lax.axis_size("ctx")
    return [term.reshape(dp_size, ctx_size, -1) for term in terms]


def reduce_at_end(terms):
    blocks = owner_blocks(terms)
    moved = (
        lax.all_to_all(
            blocks[0].astype(jnp.bfloat16), "ctx", split_axis=1, concat_axis=1, tiled=True
        ).astype(jnp.float32),
        lax.all_to_all(
            blocks[1].astype(jnp.bfloat16), "ctx", split_axis=1, concat_axis=1, tiled=True
        ).astype(jnp.float32),
        lax.all_to_all(
            blocks[2].astype(jnp.bfloat16), "ctx", split_axis=1, concat_axis=1, tiled=True
        ).astype(jnp.float32),
        lax.all_to_all(
            blocks[3].astype(jnp.bfloat16), "ctx", split_axis=1, concat_axis=1, tiled=True
        ).astype(jnp.float32),
        lax.all_to_all(
            blocks[4].astype(jnp.bfloat16), "ctx", split_axis=1, concat_axis=1, tiled=True
        ).astype(jnp.float32),
        lax.all_to_all(
            blocks[5].astype(jnp.bfloat16), "ctx", split_axis=1, concat_axis=1, tiled=True
        ).astype(jnp.float32),
        lax.all_to_all(
            blocks[6].astype(jnp.bfloat16), "ctx", split_axis=1, concat_axis=1, tiled=True
        ).astype(jnp.float32),
    )
    summed = [jnp.sum(piece, axis=1) for piece in moved]
    owned = (
        lax.psum_scatter(
            summed[0].astype(jnp.bfloat16), "dp", scatter_dimension=0, tiled=True
        ).astype(jnp.float32),
        lax.psum_scatter(
            summed[1].astype(jnp.bfloat16), "dp", scatter_dimension=0, tiled=True
        ).astype(jnp.float32),
        lax.psum_scatter(
            summed[2].astype(jnp.bfloat16), "dp", scatter_dimension=0, tiled=True
        ).astype(jnp.float32),
        lax.psum_scatter(
            summed[3].astype(jnp.bfloat16), "dp", scatter_dimension=0, tiled=True
        ).astype(jnp.float32),
        lax.psum_scatter(
            summed[4].astype(jnp.bfloat16), "dp", scatter_dimension=0, tiled=True
        ).astype(jnp.float32),
        lax.psum_scatter(
            summed[5].astype(jnp.bfloat16), "dp", scatter_dimension=0, tiled=True
        ).astype(jnp.float32),
        lax.psum_scatter(
            summed[6].astype(jnp.bfloat16), "dp", scatter_dimension=0, tiled=True
        ).astype(jnp.float32),
    )
    return [piece.reshape(-1) for piece in owned]


def body(
    tokens,
    segment_ids,
    positions,
    norm_attn,
    w_query,
    w_key,
    w_value,
    w_out,
    norm_ffn,
    w_gate,
    w_up,
    w_down,
    cotangent,
):
    seq_local, block_len, width = tokens.shape
    micro_seqs = seq_local // MICRO
    groups = HEADS // KV_HEADS
    attn_width = HEADS * HEAD_DIM
    kv_width = KV_HEADS * HEAD_DIM
    length = block_len * lax.axis_size("ctx")
    rows = micro_seqs * block_len
    score_scale = HEAD_DIM ** (-0.5)
    query_index = lax.axis_index("ctx") * block_len + jnp.arange(block_len, dtype=jnp.int32)
    key_index = jnp.arange(length, dtype=jnp.int32)
    shapes = (
        (D, attn_width),
        (D, kv_width),
        (D, kv_width),
        (attn_width, D),
        (D, FF),
        (D, FF),
        (FF, D),
    )

    def forward_weights():
        flats = (
            lax.all_gather(w_query, ("dp", "ctx"), axis=0, tiled=True),
            lax.all_gather(w_key, ("dp", "ctx"), axis=0, tiled=True),
            lax.all_gather(w_value, ("dp", "ctx"), axis=0, tiled=True),
            lax.all_gather(w_out, ("dp", "ctx"), axis=0, tiled=True),
            lax.all_gather(w_gate, ("dp", "ctx"), axis=0, tiled=True),
            lax.all_gather(w_up, ("dp", "ctx"), axis=0, tiled=True),
            lax.all_gather(w_down, ("dp", "ctx"), axis=0, tiled=True),
        )
        return [flat.reshape(shape) for flat, shape in zip(flats, shapes)]

    def backward_weights():
        flats = (
            lax.all_gather(w_query, ("dp", "ctx"), axis=0, tiled=True),
            lax.all_gather(w_key, ("dp", "ctx"), axis=0, tiled=True),
            lax.all_gather(w_value, ("dp", "ctx"), axis=0, tiled=True),
            lax.all_gather(w_out, ("dp", "ctx"), axis=0, tiled=True),
            lax.all_gather(w_gate, ("dp", "ctx"), axis=0, tiled=True),
            lax.all_gather(w_up, ("dp", "ctx"), axis=0, tiled=True),
            lax.all_gather(w_down, ("dp", "ctx"), axis=0, tiled=True),
        )
        return [flat.reshape(shape) for flat, shape in zip(flats, shapes)]

    grad_totals = [jnp.zeros(shape, jnp.float32) for shape in shapes]
    shard_totals = [
        jnp.zeros(shard.shape, jnp.float32)
        for shard in (w_query, w_key, w_value, w_out, w_gate, w_up, w_down)
    ]
    attn_gain_total = jnp.zeros((D,), jnp.float32)
    ffn_gain_total = jnp.zeros((D,), jnp.float32)
    outputs = []
    input_grads = []
    for micro in range(MICRO):
        lower = micro * micro_seqs
        upper = lower + micro_seqs
        inputs = tokens[lower:upper].astype(jnp.float32).reshape(rows, D)
        segment_part = segment_ids[lower:upper]
        position_part = positions[lower:upper]
        grad_out = cotangent[lower:upper].astype(jnp.float32).reshape(rows, D)
        query_weight, key_weight, value_weight, out_weight, gate_weight, up_weight, down_weight = (
            forward_weights()
        )
        scale_attn = rms_scale(inputs)
        normed_attn = (inputs * scale_attn * norm_attn).astype(jnp.bfloat16)
        cosine, sine = rope_tables(position_part)
        query_rot = rotate(
            product(normed_attn, query_weight).reshape(micro_seqs, block_len, HEADS, HEAD_DIM),
            cosine,
            sine,
        ).astype(jnp.bfloat16)
        key_rot = (
            rotate(
                product(normed_attn, key_weight).reshape(micro_seqs, block_len, KV_HEADS, HEAD_DIM),
                cosine,
                sine,
            )
            .astype(jnp.bfloat16)
            .reshape(micro_seqs, block_len, kv_width)
        )
        value_low = (
            product(normed_attn, value_weight)
            .astype(jnp.bfloat16)
            .reshape(micro_seqs, block_len, kv_width)
        )
        key_all, value_all, segment_all = (
            lax.all_gather(key_rot, "ctx", axis=1, tiled=True),
            lax.all_gather(value_low, "ctx", axis=1, tiled=True),
            lax.all_gather(segment_part, "ctx", axis=1, tiled=True),
        )
        key_heads = key_all.reshape(micro_seqs, length, KV_HEADS, HEAD_DIM)
        value_heads = value_all.reshape(micro_seqs, length, KV_HEADS, HEAD_DIM)
        query_groups = query_rot.reshape(micro_seqs, block_len, KV_HEADS, groups, HEAD_DIM)
        allowed = (
            (segment_part[:, :, None] == segment_all[:, None, :])
            & (key_index[None, None, :] <= query_index[None, :, None])
        )[:, None, None]
        masked = masked_scores(query_groups, key_heads, allowed, score_scale)
        row_max = jnp.max(masked, axis=-1, keepdims=True)
        exponent = jnp.exp(masked - row_max)
        total = jnp.sum(exponent, axis=-1, keepdims=True)
        probs_low = (exponent / total).astype(jnp.bfloat16)
        log_total = row_max + jnp.log(total)
        attended = (
            jnp.einsum(
                "skgcl,slkd->sckgd", probs_low, value_heads, preferred_element_type=jnp.float32
            )
            .astype(jnp.bfloat16)
            .reshape(rows, attn_width)
        )
        resid = inputs + product(attended, out_weight)
        scale_ffn = rms_scale(resid)
        normed_ffn = (resid * scale_ffn * norm_ffn).astype(jnp.bfloat16)
        gate = product(normed_ffn, gate_weight)
        up = product(normed_ffn, up_weight)
        hidden = (jax.nn.silu(gate) * up).astype(jnp.bfloat16)
        outputs.append(
            (resid + product(hidden, down_weight))
            .astype(jnp.bfloat16)
            .reshape(micro_seqs, block_len, D)
        )
        query_weight, key_weight, value_weight, out_weight, gate_weight, up_weight, down_weight = (
            backward_weights()
        )
        down_grad = grad_out.astype(jnp.bfloat16)
        fresh_down = product_left(hidden, down_grad)
        hidden_grad = product_right(down_grad, down_weight)
        gate_sigmoid = jax.nn.sigmoid(gate)
        gate_grad = (hidden_grad * up * gate_sigmoid * (1.0 + gate * (1.0 - gate_sigmoid))).astype(
            jnp.bfloat16
        )
        up_grad = (hidden_grad * gate * gate_sigmoid).astype(jnp.bfloat16)
        fresh_gate = product_left(normed_ffn, gate_grad)
        fresh_up = product_left(normed_ffn, up_grad)
        normed_grad = product_right(gate_grad, gate_weight) + product_right(up_grad, up_weight)
        resid_grad, ffn_gain_grad = norm_back(resid, scale_ffn, norm_ffn, normed_grad)
        resid_grad = resid_grad + grad_out
        branch_grad = resid_grad.astype(jnp.bfloat16)
        fresh_out = product_left(attended, branch_grad)
        attended_grad = (
            product_right(branch_grad, out_weight)
            .astype(jnp.bfloat16)
            .reshape(micro_seqs, block_len, KV_HEADS, groups, HEAD_DIM)
        )
        probs = jnp.exp(masked_scores(query_groups, key_heads, allowed, score_scale) - log_total)
        probs_grad = jnp.einsum(
            "sckgd,slkd->skgcl", attended_grad, value_heads, preferred_element_type=jnp.float32
        )
        inner = jnp.sum(probs * probs_grad, axis=-1, keepdims=True)
        scores_grad = (probs * (probs_grad - inner)).astype(jnp.bfloat16)
        query_grad = (
            jnp.einsum(
                "skgcl,slkd->sckgd", scores_grad, key_heads, preferred_element_type=jnp.float32
            )
            * score_scale
        )
        key_part = (
            jnp.einsum(
                "skgcl,sckgd->slkd", scores_grad, query_groups, preferred_element_type=jnp.float32
            )
            * score_scale
        )
        value_part = jnp.einsum(
            "skgcl,sckgd->slkd",
            probs.astype(jnp.bfloat16),
            attended_grad,
            preferred_element_type=jnp.float32,
        )
        key_grad, value_grad = (
            lax.psum_scatter(
                key_part.reshape(micro_seqs, length, kv_width).astype(jnp.bfloat16),
                "ctx",
                scatter_dimension=1,
                tiled=True,
            ).astype(jnp.float32),
            lax.psum_scatter(
                value_part.reshape(micro_seqs, length, kv_width).astype(jnp.bfloat16),
                "ctx",
                scatter_dimension=1,
                tiled=True,
            ).astype(jnp.float32),
        )
        query_low = (
            rotate_back(query_grad.reshape(micro_seqs, block_len, HEADS, HEAD_DIM), cosine, sine)
            .astype(jnp.bfloat16)
            .reshape(rows, attn_width)
        )
        key_low = (
            rotate_back(key_grad.reshape(micro_seqs, block_len, KV_HEADS, HEAD_DIM), cosine, sine)
            .astype(jnp.bfloat16)
            .reshape(rows, kv_width)
        )
        value_grad_low = value_grad.astype(jnp.bfloat16).reshape(rows, kv_width)
        fresh_query = product_left(normed_attn, query_low)
        fresh_key = product_left(normed_attn, key_low)
        fresh_value = product_left(normed_attn, value_grad_low)
        attn_normed_grad = (
            product_right(query_low, query_weight)
            + product_right(key_low, key_weight)
            + product_right(value_grad_low, value_weight)
        )
        input_grad, attn_gain_grad = norm_back(inputs, scale_attn, norm_attn, attn_normed_grad)
        input_grads.append((input_grad + resid_grad).reshape(micro_seqs, block_len, D))
        attn_gain_total = attn_gain_total + attn_gain_grad
        ffn_gain_total = ffn_gain_total + ffn_gain_grad
        fresh = [fresh_query, fresh_key, fresh_value, fresh_out, fresh_gate, fresh_up, fresh_down]
        grad_totals = [running + piece for running, piece in zip(grad_totals, fresh)]
    shard_totals = reduce_at_end(grad_totals)
    attn_gain_sum, ffn_gain_sum = lax.psum((attn_gain_total, ffn_gain_total), ("dp", "ctx"))
    output = jnp.concatenate(outputs, axis=0)
    d_tokens = jnp.concatenate(input_grads, axis=0)
    return (
        output,
        d_tokens,
        attn_gain_sum,
        shard_totals[0],
        shard_totals[1],
        shard_totals[2],
        shard_totals[3],
        ffn_gain_sum,
        shard_totals[4],
        shard_totals[5],
        shard_totals[6],
    )


def solution(mesh):
    in_specs = (
        P("dp", "ctx", None),
        P("dp", "ctx"),
        P("dp", "ctx"),
        P(),
        P(("dp", "ctx")),
        P(("dp", "ctx")),
        P(("dp", "ctx")),
        P(("dp", "ctx")),
        P(),
        P(("dp", "ctx")),
        P(("dp", "ctx")),
        P(("dp", "ctx")),
        P("dp", "ctx", None),
    )
    out_specs = (
        P("dp", "ctx", None),
        P("dp", "ctx", None),
        P(),
        P(("dp", "ctx")),
        P(("dp", "ctx")),
        P(("dp", "ctx")),
        P(("dp", "ctx")),
        P(),
        P(("dp", "ctx")),
        P(("dp", "ctx")),
        P(("dp", "ctx")),
    )
    return jax.shard_map(body, mesh=mesh, in_specs=in_specs, out_specs=out_specs, check_vma=False)
```

profile of v0, /device:TPU:0, one launch (start us, length us, event | category | flops | bytes accessed | tf_op | source)
XLA Modules:
  0.0 967.7 jit_solution(10681395734420961702)
XLA Ops:
  13.2 47.4 %all-gather.4 = bf16[32,1,9600]{2,1,0:T(2,128)(2,1)S(1)} all-gather(bf16[1,1,9600]{2,1,0:T(2,128)(2,1)S(1)} %reshape.1609), channel_id=1, replica_groups=mesh['dp'=8,'ctx'=4] {'dp','ctx'}, dimensions={0}, use_global_device_ids=true | all-gather | bytes 633600 | tf_op jit(solution)/shard_map/all_gather | solution.py:168
  60.6 3.7 reduce.13
  66.2 42.0 %all-gather.5 = bf16[32,1,9600]{2,1,0:T(2,128)(2,1)S(1)} all-gather(bf16[1,1,9600]{2,1,0:T(2,128)(2,1)S(1)} %reshape.1611), channel_id=1, replica_groups=mesh['dp'=8,'ctx'=4] {'dp','ctx'}, dimensions={0}, use_global_device_ids=true | all-gather | bytes 633600 | tf_op jit(solution)/shard_map/all_gather | solution.py:167
  108.2 3.7 reduce.14
  117.0 8.5 all-gather.2
  126.8 10.4 %all-gather.3 = bf16[1024,320]{0,1:T(8,128)(2,1)S(1)} all-gather(bf16[256,320]{0,1:T(8,128)(2,1)S(1)} %fusion.106), channel_id=5, replica_groups=mesh['dp'=8,'ctx'=4] {'ctx'}, dimensions={0}, use_global_device_ids=true | all-gather | bytes 819200 | tf_op jit(solution)/shard_map/all_gather | solution.py:230
  137.3 5.1 all_gather.32
  142.3 5.1 all_gather.76
  147.4 8.4 all-gather
  155.9 8.7 all-gather.1
  166.0 39.5 %reduce.15 = bf16[32,28800]{1,0:T(8,128)(2,1)S(1)} reduce(bf16[32,1,28800]{2,1,0:T(2,128)(2,1)} %all-gather.20.cloned.1.call-done, bf16[]{:T(256)} %constant.80), dimensions={1}, to_apply=%all-gather.6.reduce_sub_computation | reduce | bytes 3686402 | tf_op jit(solution)/shard_map/all_gather | solution.py:166
  211.4 6.8 fusion.151
  218.2 7.7 fusion.6
  225.9 39.9 %reduce.16 = bf16[32,28800]{1,0:T(8,128)(2,1)S(1)} reduce(bf16[32,1,28800]{2,1,0:T(2,128)(2,1)} %all-gather.22.cloned.1.call-done, bf16[]{:T(256)} %constant.80), dimensions={1}, to_apply=%all-gather.7.reduce_sub_computation | reduce | bytes 3686402 | tf_op jit(solution)/shard_map/all_gather | solution.py:169
  268.6 8.7 fusion.44
  280.5 7.0 fusion.150
  287.5 7.6 fusion.7
  295.2 7.0 fusion.47
  304.5 10.0 %reshape.1537 = bf16[960,2560]{1,0:T(8,128)(2,1)} reshape(bf16[2457600]{0:T(1024)(128)(2,1)} %all-gather.14.cloned.1.call-done) | data formatting | bytes 9830400 | tf_op jit(solution)/shard_map/reshape | solution.py:174
  314.5 10.0 %reshape.1538 = bf16[960,2560]{1,0:T(8,128)(2,1)} reshape(bf16[2457600]{0:T(1024)(128)(2,1)} %all-gather.16.cloned.1.call-done) | data formatting | bytes 9830400 | tf_op jit(solution)/shard_map/reshape | solution.py:174
  324.4 5.6 fusion.152
  333.1 10.4 %all-gather.18.cloned.1.call-done = bf16[2457600]{0:T(1024)(128)(2,1)} async-done(((bf16[76800]{0:T(1024)(128)(2,1)}), bf16[2457600]{0:T(1024)(128)(2,1)}) %all-gather.18.cloned.1.call-update) | async-done | bytes 4915216 | tf_op jit(solution)/shard_map/all_gather | solution.py:172
  343.5 9.6 reshape.1539
  353.0 9.0 multiply_convert_fusion.2
  362.1 4.8 fusion.156
  373.4 4.1 multiply_convert_fusion
  386.4 8.4 fusion
  394.7 7.9 fusion.17
  411.1 13.0 %fusion.3 = (f32[5,3,256]{2,1,0:T(4,128)S(1)}, f32[5,1024,256,3]{2,1,3,0:T(8,128)}) fusion(f32[1,5,3,256,1024]{3,4,2,1,0:T(8,128)} %get-tuple-element.82, f32[5,3,256]{2,1,0:T(4,128)S(1)} %log_add_fusion.1, bf16[1024,5,64,1]{0,2,3,1:T(8,128)(2,1)} %bitcast.417, bf16[256,5,3,64]{0,3,2,1:T(8,128)(2,1)S(1)} %bitcast.406), kind=kOutput, calls=%fused_computation.9 | convolution fusion | flops 515109120 | bytes 32634880 | tf_op jit(solution)/shard_map/sckgd,slkd->skgcl/dot_general | solution.py:289
  427.1 7.7 fusion.16
  448.0 9.1 fusion.37
  457.1 4.4 add_convert_fusion.4
  461.5 3.8 fusion.111
  465.3 5.2 convert_element_type.480
  473.5 4.4 all-to-all-start
  478.4 9.1 fusion.34
  489.6 5.3 convert_element_type.486
  497.8 6.6 fusion.158
  506.5 4.4 all-to-all-start.3
  514.3 23.1 %all-to-all-done.3 = bf16[8,4,28800]{2,0,1:T(8,128)(2,1)} async-done(((bf16[8,4,28800]{2,0,1:T(8,128)(2,1)}), bf16[8,4,28800]{2,0,1:T(8,128)(2,1)}, u32[]{:S(2)}, u32[]{:S(2)}) %all-to-all-start.3) | async-done | bytes 1843232 | tf_op jit(solution)/shard_map/all_to_all | solution.py:89
  537.4 4.1 all-to-all-start.1
  551.5 3.7 all-to-all-start.2
  555.1 7.9 add_convert_fusion.2
  563.0 8.1 convert_element_type.488
  571.1 6.1 copy.57
  577.2 5.0 all-to-all-start.4
  588.7 8.1 convert_element_type.490
  596.8 6.0 copy.58
  602.7 35.4 %all-to-all-done.4 = bf16[8,4,76800]{2,0,1:T(8,128)(2,1)} async-done(((bf16[8,4,76800]{2,0,1:T(8,128)(2,1)}), bf16[8,4,76800]{2,0,1:T(8,128)(2,1)}, u32[]{:S(2)}, u32[]{:S(2)}) %all-to-all-start.4) | async-done | bytes 4915232 | tf_op jit(solution)/shard_map/all_to_all | solution.py:92
  638.1 5.0 all-to-all-start.5
  646.0 3.7 add_convert_fusion
  649.7 7.9 copy.59
  657.6 10.0 %convert_element_type.492 = bf16[8,4,76800]{2,1,0:T(4,128)(2,1)} reshape(bf16[2560,960]{1,0:T(8,128)(2,1)} %copy.59) | data formatting | bytes 9830400 | tf_op jit(solution)/shard_map/convert_element_type | solution.py:99
  667.5 6.1 copy.60
  673.6 25.5 %all-to-all-done.5 = bf16[8,4,76800]{2,0,1:T(8,128)(2,1)} async-done(((bf16[8,4,76800]{2,0,1:T(8,128)(2,1)}), bf16[8,4,76800]{2,0,1:T(8,128)(2,1)}, u32[]{:S(2)}, u32[]{:S(2)}) %all-to-all-start.5) | async-done | bytes 4915232 | tf_op jit(solution)/shard_map/all_to_all | solution.py:95
  699.1 5.0 all-to-all-start.6
  712.3 4.5 reduce_sum.248
  716.8 4.5 reduce_sum.249
  721.3 38.7 %all-to-all-done.6 = bf16[8,4,76800]{2,0,1:T(8,128)(2,1)} async-done(((bf16[8,4,76800]{2,0,1:T(8,128)(2,1)}), bf16[8,4,76800]{2,0,1:T(8,128)(2,1)}, u32[]{:S(2)}, u32[]{:S(2)}) %all-to-all-start.6) | async-done | bytes 4915232 | tf_op jit(solution)/shard_map/all_to_all | solution.py:98
  760.0 4.5 reduce_sum.250
  765.9 5.2 fusion.58
  771.1 4.8 fusion.59
  783.1 45.0 %all-reduce.7 = (f32[960]{0:T(1024)}, f32[960]{0:T(1024)}) all-reduce(f32[960]{0:T(1024)S(1)} %add.336, f32[960]{0:T(1024)S(1)} %add.341), channel_id=1, replica_groups=mesh['dp'=8,'ctx'=4] {'dp','ctx'}, use_global_device_ids=true, to_apply=%region_20.21 | all-reduce | flops 1920 | bytes 15360 | tf_op jit(solution)/shard_map/psum | solution.py:352
  831.8 109.9 %all-reduce.11.cloned.1.call-done = (bf16[8,28800]{1,0:T(8,128)(2,1)}, bf16[8,9600]{1,0:T(8,128)(2,1)}, bf16[8,9600]{1,0:T(8,128)(2,1)}, bf16[8,28800]{1,0:T(8,1...) async-done(((bf16[8,28800]{1,0:T(8,128)(2,1)}, bf16[8,9600]{1,0:T(8,128)(2,1)}, bf16[8,9600]{1,0:T(8,128)(2,1)}, ...) | async-done | bytes 4915216
  (359 shorter events, 144.1 us)
Async XLA Ops:
  7.2 58.8 %copy-start.1 = (bf16[2,256,960]{1,2,0:T(8,128)(2,1)S(1)}, bf16[2,256,960]{1,2,0:T(8,128)(2,1)}, u32[]{:S(2)}) copy-start(bf16[2,256,960]{1,2,0:T(8,128)(2,1)} %param.13) | copy-start | bytes 2949124
  7.2 59.0 %copy-start.85 = (bf16[9600]{0:T(1024)(128)(2,1)S(1)}, bf16[9600]{0:T(1024)(128)(2,1)}, u32[]{:S(2)}) copy-start(bf16[9600]{0:T(1024)(128)(2,1)} %param.18) | copy-start | bytes 57604
  7.2 158.8 %all-gather.20.cloned.1.call-start = ((), (), s32[]{:S(2)}) async-start(), calls=%async_computation.18 | async-start | bytes 3801600 | tf_op jit(solution)/shard_map/all_gather | solution.py:166
  8.9 217.0 %all-gather.22.cloned.1.call-start = ((), (), s32[]{:S(2)}) async-start(), calls=%async_computation.19 | async-start | bytes 3801600 | tf_op jit(solution)/shard_map/all_gather | solution.py:169
  10.5 294.0 %all-gather.14.cloned.1.call-start = ((), (), s32[]{:S(2)}) async-start(), calls=%async_computation.11 | async-start | bytes 5068800 | tf_op jit(solution)/shard_map/all_gather | solution.py:170
  11.2 303.2 %all-gather.16.cloned.1.call-start = ((), (), s32[]{:S(2)}) async-start(), calls=%async_computation.12 | async-start | bytes 5068800 | tf_op jit(solution)/shard_map/all_gather | solution.py:171
  11.8 331.7 %all-gather.18.cloned.1.call-start = ((), (), s32[]{:S(2)}) async-start(), calls=%async_computation.13 | async-start | bytes 5068800 | tf_op jit(solution)/shard_map/all_gather | solution.py:172
  12.4 492.0 %reduce-scatter.9.cloned.1.call-start = ((), (), s32[]{:S(2)}) async-start(), calls=%async_computation.16 | async-start | bytes 819200 | tf_op jit(solution)/shard_map/reduce_scatter | solution.py:313
  60.6 52.8 %copy-start.72 = (f32[960]{0:T(1024)S(1)}, f32[960]{0:T(1024)}, u32[]{:S(2)}) copy-start(f32[960]{0:T(1024)} %param.16) | copy-start | bytes 11524
  113.4 94.9 %copy-start.80 = (f32[256]{0:T(256)}, f32[256]{0:T(256)S(1)}, u32[]{:S(2)}) copy-start(f32[256]{0:T(256)S(1)} %get-tuple-element.94) | copy-start | bytes 3076
  115.1 10.4 %copy-start.90 = (s32[2,256]{1,0:T(2,128)S(1)}, s32[2,256]{1,0:T(2,128)}, u32[]{:S(2)}) copy-start(s32[2,256]{1,0:T(2,128)} %param.15) | copy-start | bytes 6148
  115.8 21.5 %copy-start.91 = (s32[2,256]{1,0:T(2,128)S(1)}, s32[2,256]{1,0:T(2,128)}, u32[]{:S(2)}) copy-start(s32[2,256]{1,0:T(2,128)} %param.14) | copy-start | bytes 6148
  126.2 39.8 %copy-start.49 = (f32[256,64]{0,1:T(8,128)}, f32[256,64]{0,1:T(8,128)S(1)}, u32[]{:S(2)}) copy-start(f32[256,64]{0,1:T(8,128)S(1)} %get-tuple-element.58) | copy-start | bytes 196612
  126.2 85.0 %copy-start.45 = (f32[256,64]{0,1:T(8,128)}, f32[256,64]{0,1:T(8,128)S(1)}, u32[]{:S(2)}) copy-start(f32[256,64]{0,1:T(8,128)S(1)} %get-tuple-element.59) | copy-start | bytes 196612
  137.3 143.2 %copy-start.14 = (bf16[1024,320]{0,1:T(8,128)(2,1)}, bf16[1024,320]{0,1:T(8,128)(2,1)S(1)}, u32[]{:S(2)}) copy-start(bf16[1024,320]{0,1:T(8,128)(2,1)S(1)} %all-gather.3) | copy-start | bytes 1966084
  211.4 6.8 copy-start.20
  218.2 50.4 %copy-start.74 = (f32[5,3,256]{2,1,0:T(4,128)}, f32[5,3,256]{2,1,0:T(4,128)S(1)}, u32[]{:S(2)}) copy-start(f32[5,3,256]{2,1,0:T(4,128)S(1)} %get-tuple-element.81) | copy-start | bytes 46084
  225.9 42.7 %copy-start.77 = (f32[5,3,256]{2,1,0:T(4,128)}, f32[5,3,256]{2,1,0:T(4,128)S(1)}, u32[]{:S(2)}) copy-start(f32[5,3,256]{2,1,0:T(4,128)S(1)} %fusion.6) | copy-start | bytes 46084
  268.6 8.7 copy-start.2
  278.3 26.0 %copy-start.11 = (f32[256,960]{0,1:T(8,128)}, f32[256,960]{0,1:T(8,128)S(1)}, u32[]{:S(2)}) copy-start(f32[256,960]{0,1:T(8,128)S(1)} %get-tuple-element.84) | copy-start | bytes 2949124
  280.4 7.1 copy-start.22
  287.5 7.7 copy-start.25
  324.4 5.6 copy-start
  333.1 19.9 %copy-start.26 = (bf16[2,256,960]{1,2,0:T(8,128)(2,1)S(1)}, bf16[2,256,960]{1,2,0:T(8,128)(2,1)}, u32[]{:S(2)}) copy-start(bf16[2,256,960]{1,2,0:T(8,128)(2,1)} %param.25) | copy-start | bytes 2949124
  343.5 23.5 %slice-start.8 = ((s8[4915200]{0:T(1024)(128)(4,1)}), s8[720896]{0:T(1024)(128)(4,1)S(1)}, s32[]{:S(2)}) async-start(s8[4915200]{0:T(1024)(128)(4,1)} %bitcast.400), calls=%async_computation.29 | async-start | bytes 1441792
  353.0 14.0 %slice-start.9 = ((s8[4915200]{0:T(1024)(128)(4,1)}), s8[4194304]{0:T(1024)(128)(4,1)S(1)}, s32[]{:S(2)}) async-start(s8[4915200]{0:T(1024)(128)(4,1)} %bitcast.400), calls=%async_computation.30 | async-start | bytes 8388608
  362.1 4.9 copy-start.12
  362.1 8.1 slice-start.10
  377.6 8.0 slice-start.4
  379.7 5.9 slice-start.5
  379.7 5.9 slice-start.6
  394.7 7.9 copy-start.15
  408.5 96.9 %reduce-scatter.5.cloned.1.call-start = ((), (), s32[]{:S(2)}) async-start(), calls=%async_computation.14 | async-start | bytes 819200 | tf_op jit(solution)/shard_map/reduce_scatter | solution.py:313
  411.1 13.1 %slice-start = ((s8[15728640]{0:T(1024)(128)(4,1)}), s8[4194304]{0:T(1024)(128)(4,1)S(1)}, s32[]{:S(2)}) async-start(s8[15728640]{0:T(1024)(128)(4,1)} %bitcast.396), calls=%async_computation.21 | async-start | bytes 8388608
  411.1 13.7 %slice-start.1 = ((s8[15728640]{0:T(1024)(128)(4,1)}), s8[4194304]{0:T(1024)(128)(4,1)S(1)}, s32[]{:S(2)}) async-start(s8[15728640]{0:T(1024)(128)(4,1)} %bitcast.396), calls=%async_computation.22 | async-start | bytes 8388608
  411.1 15.2 %slice-start.2 = ((s8[15728640]{0:T(1024)(128)(4,1)}), s8[4194304]{0:T(1024)(128)(4,1)S(1)}, s32[]{:S(2)}) async-start(s8[15728640]{0:T(1024)(128)(4,1)} %bitcast.396), calls=%async_computation.23 | async-start | bytes 8388608
  411.1 16.0 %slice-start.3 = ((s8[15728640]{0:T(1024)(128)(4,1)}), s8[3145728]{0:T(1024)(128)(4,1)S(1)}, s32[]{:S(2)}) async-start(s8[15728640]{0:T(1024)(128)(4,1)} %bitcast.396), calls=%async_computation.24 | async-start | bytes 6291456
  427.1 7.7 copy-start.17
  439.6 5.9 copy-start.73
  439.6 5.9 copy-start.81
  442.9 98.7 %reduce-scatter.7.cloned.1.call-start = ((), (), s32[]{:S(2)}) async-start(), calls=%async_computation.15 | async-start | bytes 819200 | tf_op jit(solution)/shard_map/reduce_scatter | solution.py:319
  448.0 9.1 copy-start.84
  473.5 32.9 %all-to-all-start = ((bf16[8,4,28800]{2,0,1:T(8,128)(2,1)}), bf16[8,4,28800]{2,0,1:T(8,128)(2,1)}, u32[]{:S(2)}, u32[]{:S(2)}) async-start(bf16[8,4,28800]{2,0,1:T(8,128)(2,1)} %copy.51), calls=%async_computation.4 | async-start | bytes 3686400 | tf_op jit(solution)/shard_map/all_to_all | solution.py:80
  477.9 9.6 copy-start.69
  477.9 66.1 %reduce-scatter.11.cloned.1.call-start = ((), (), s32[]{:S(2)}) async-start(), calls=%async_computation.17 | async-start | bytes 819200 | tf_op jit(solution)/shard_map/reduce_scatter | solution.py:319
  478.4 9.2 copy-start.5
  478.4 9.2 copy-start.7
  504.4 6.5 copy-start.66
  505.4 5.6 copy-start.67
  506.5 31.0 %all-to-all-start.3 = ((bf16[8,4,28800]{2,0,1:T(8,128)(2,1)}), bf16[8,4,28800]{2,0,1:T(8,128)(2,1)}, u32[]{:S(2)}, u32[]{:S(2)}) async-start(bf16[8,4,28800]{2,0,1:T(8,128)(2,1)} %copy.56), calls=%async_computation.7 | async-start | bytes 3686400 | tf_op jit(solution)/shard_map/all_to_all | solution.py:89
  537.4 14.0 %all-to-all-start.1 = ((bf16[8,4,9600]{2,0,1:T(8,128)(2,1)}), bf16[8,4,9600]{2,0,1:T(8,128)(2,1)}, u32[]{:S(2)}, u32[]{:S(2)}) async-start(bf16[8,4,9600]{2,0,1:T(8,128)(2,1)} %copy.53), calls=%async_computation.5 | async-start | bytes 1228800 | tf_op jit(solution)/shard_map/all_to_all | solution.py:83
  551.5 25.7 %all-to-all-start.2 = ((bf16[8,4,9600]{2,0,1:T(8,128)(2,1)}), bf16[8,4,9600]{2,0,1:T(8,128)(2,1)S(1)}, u32[]{:S(2)}, u32[]{:S(2)}) async-start(bf16[8,4,9600]{2,0,1:T(8,128)(2,1)} %copy.55), calls=%async_computation.6 | async-start | bytes 1228800 | tf_op jit(solution)/shard_map/all_to_all | solution.py:86
  577.2 60.9 %all-to-all-start.4 = ((bf16[8,4,76800]{2,0,1:T(8,128)(2,1)}), bf16[8,4,76800]{2,0,1:T(8,128)(2,1)}, u32[]{:S(2)}, u32[]{:S(2)}) async-start(bf16[8,4,76800]{2,0,1:T(8,128)(2,1)} %copy.57), calls=%async_computation.8 | async-start | bytes 9830400 | tf_op jit(solution)/shard_map/all_to_all | solution.py:92
  602.7 40.4 %copy-start.29 = (bf16[2,256,960]{1,2,0:T(8,128)(2,1)S(1)}, bf16[2,256,960]{1,2,0:T(8,128)(2,1)}, u32[]{:S(2)}) copy-start(bf16[2,256,960]{1,2,0:T(8,128)(2,1)} %param.25) | copy-start | bytes 2949124
  638.1 61.0 %all-to-all-start.5 = ((bf16[8,4,76800]{2,0,1:T(8,128)(2,1)}), bf16[8,4,76800]{2,0,1:T(8,128)(2,1)}, u32[]{:S(2)}, u32[]{:S(2)}) async-start(bf16[8,4,76800]{2,0,1:T(8,128)(2,1)} %copy.58), calls=%async_computation.9 | async-start | bytes 9830400 | tf_op jit(solution)/shard_map/all_to_all | solution.py:95
  699.1 61.0 %all-to-all-start.6 = ((bf16[8,4,76800]{2,0,1:T(8,128)(2,1)}), bf16[8,4,76800]{2,0,1:T(8,128)(2,1)}, u32[]{:S(2)}, u32[]{:S(2)}) async-start(bf16[8,4,76800]{2,0,1:T(8,128)(2,1)} %copy.60), calls=%async_computation.10 | async-start | bytes 9830400 | tf_op jit(solution)/shard_map/all_to_all | solution.py:98
  704.1 237.6 %all-reduce.11.cloned.1.call-start = ((), (), s32[]{:S(2)}) async-start(), calls=%async_computation.20 | async-start | bytes 9830400
  765.9 5.2 copy-start.13
  765.9 5.2 copy-start.63
  771.1 5.9 copy-start.40
  771.1 5.9 copy-start.44
  780.0 48.1 %copy-start.6 = (f32[256,960]{0,1:T(8,128)S(1)}, f32[256,960]{0,1:T(8,128)}, u32[]{:S(2)}) copy-start(f32[256,960]{0,1:T(8,128)} %copy-done.4) | copy-start | bytes 2949124
  780.0 48.1 %copy-start.87 = (f32[256]{0:T(256)S(1)}, f32[256]{0:T(256)}, u32[]{:S(2)}) copy-start(f32[256]{0:T(256)} %get-tuple-element.69) | copy-start | bytes 3076
  780.0 48.1 %copy-start.88 = (f32[256]{0:T(256)S(1)}, f32[256]{0:T(256)}, u32[]{:S(2)}) copy-start(f32[256]{0:T(256)} %get-tuple-element.95) | copy-start | bytes 3076
  (60 other events, 134.6 us)
Sparse Core Ops, SparseCore 0:
  11.5 66.7 all-gather.19
  81.8 60.0 all-gather.21
  144.7 66.9 all-gather.13
  214.3 63.1 all-gather.15
  280.2 63.2 all-gather.17
  408.7 21.2 reduce-scatter.8
  443.0 21.2 reduce-scatter.4
  466.9 26.0 reduce-scatter.6
  497.9 26.2 reduce-scatter.10
  764.7 176.9 all-reduce.10
where the time goes:
time: 976 us; the launch traced here: 968 us
  waiting for transfers between devices  249 us (26%)
  matrix products  188 us (19%)
  blocking collectives  180 us (18%)
  other arithmetic  175 us (18%)
  local copies, waits for them, and re-layouts  126 us (13%)
  starting transfers between devices  32.6 us (3%)
  between operations  16 us (2%)
    unnamed x11, waiting for transfers between devices  112 us
    all_gather x1, blocking collectives, forward_weights(): lax.all_gather(w_value, ('dp', 'ctx'), axis=0, tiled=True)  47.4 us
    dot_general x14, matrix products, product_left(): lax.dot_general(left, right, (((0,), (0,)), ((), ())), preferred_element_...  45.5 us
    psum x1, blocking collectives, body(): lax.psum((attn_gain_total, ffn_gain_total), ('dp', 'ctx'))  45 us
    all_gather x1, blocking collectives, forward_weights(): lax.all_gather(w_key, ('dp', 'ctx'), axis=0, tiled=True)  42 us
    all_gather x1, other arithmetic, forward_weights(): lax.all_gather(w_out, ('dp', 'ctx'), axis=0, tiled=True)  39.9 us
    all_gather x1, other arithmetic, forward_weights(): lax.all_gather(w_query, ('dp', 'ctx'), axis=0, tiled=True)  39.5 us
    all_to_all x1, waiting for transfers between devices, reduce_at_end(): lax.all_to_all(blocks[6].astype(jnp.bfloat16), 'ctx', split_axis=1, conca...  38.7 us
  transfers between devices with their start and end apart: 17, of which 7 were waited for; matrix products, arithmetic and copies ran while one was open for 40% of the time, Pallas kernels for 0%

commit v1 on v0

--- a/solution.py
+++ b/solution.py
@@ -14,6 +14,28 @@
 mask_fill = -1000000000.0
 
 
+def cut_along(array, dim, length):
+    before, after = (array.shape[:dim], array.shape[dim + 1 :])
+    return jnp.moveaxis(array.reshape(*before, length, -1, *after), dim, 0)
+
+
+def joined_along(tiles, dim):
+    dims = list(tiles.shape[1:])
+    dims[dim] *= tiles.shape[0]
+    return jnp.moveaxis(tiles, 0, dim).reshape(dims)
+
+
+def pairwise_exchange(x, axis, split_dim, concat_dim):
+    peers, place = (lax.axis_size(axis), lax.axis_index(axis))
+    parts = cut_along(x, split_dim, peers)
+    outs = [parts[place]]
+    for step in range(1, peers):
+        sent = parts[place ^ step]
+        outs.append(lax.ppermute(sent, axis, [(i, i ^ step) for i in range(peers)]))
+    parts = jnp.stack(outs)[place ^ jnp.arange(peers)]
+    return joined_along(parts, concat_dim)
+
+
 def rms_scale(values):
     return lax.rsqrt(jnp.mean(values * values, axis=-1, keepdims=True) + norm_eps)
 
@@ -92,9 +114,7 @@
         lax.all_to_all(
             blocks[4].astype(jnp.bfloat16), "ctx", split_axis=1, concat_axis=1, tiled=True
         ).astype(jnp.float32),
-        lax.all_to_all(
-            blocks[5].astype(jnp.bfloat16), "ctx", split_axis=1, concat_axis=1, tiled=True
-        ).astype(jnp.float32),
+        pairwise_exchange(blocks[5].astype(jnp.bfloat16), "ctx", 1, 1).astype(jnp.float32),
         lax.all_to_all(
             blocks[6].astype(jnp.bfloat16), "ctx", split_axis=1, concat_axis=1, tiled=True
         ).astype(jnp.float32),

time: 976 us -> 980 us (level)
  local copies, waits for them, and re-layouts: 126 us -> 145 us
  waiting for transfers between devices: 249 us -> 230 us
    ppermute x0 -> x3, waiting for transfers between devices: none -> 47.6 us  [pairwise_exchange(): outs.append(lax.ppermute(sent, axis, [(i, i ^ step) for i in range(peers)]))]
    all_to_all x1, waiting for transfers between devices: 35.4 us -> 7.12 us  [reduce_at_end(): lax.all_to_all(blocks[4].astype(jnp.bfloat16), 'ctx', split_axis=1, conca...]
    all_to_all x1 -> x0, waiting for transfers between devices: 25.5 us -> none  [reduce_at_end(): lax.all_to_all(blocks[5].astype(jnp.bfloat16), 'ctx', split_axis=1, conca...]
    all_to_all x1, waiting for transfers between devices: 38.7 us -> 24.5 us  [reduce_at_end(): lax.all_to_all(blocks[6].astype(jnp.bfloat16), 'ctx', split_axis=1, conca...]
    another operation x0 -> x1, local copies, waits for them, and re-layouts: none -> 13.4 us
    another operation x2 -> x3, other arithmetic: 15.6 us -> 21 us
  transfers between devices with their start and end apart: 17 -> 19, of which waited for: 7 -> 8; matrix products, arithmetic and copies ran while one was open for 40% -> 43% of each run, Pallas kernels for 0% -> 0%
where the time goes in v1:
time: 980 us; the launch traced here: 971 us
  waiting for transfers between devices  230 us (23%)
  matrix products  194 us (20%)
  blocking collectives  179 us (18%)
  other arithmetic  178 us (18%)
  local copies, waits for them, and re-layouts  145 us (15%)
  starting transfers between devices  29.8 us (3%)
  between operations  16 us (2%)
    unnamed x11, waiting for transfers between devices  112 us
    dot_general x14, matrix products, product_left(): lax.dot_general(left, right, (((0,), (0,)), ((), ())), preferred_element_...  48.8 us
    ppermute x3, waiting for transfers between devices, pairwise_exchange(): outs.append(lax.ppermute(sent, axis, [(i, i ^ step) for i in range(peers)]))  47.6 us
    all_gather x1, blocking collectives, forward_weights(): lax.all_gather(w_value, ('dp', 'ctx'), axis=0, tiled=True)  47.4 us
    psum x1, blocking collectives, body(): lax.psum((attn_gain_total, ffn_gain_total), ('dp', 'ctx'))  44.7 us
    all_gather x1, blocking collectives, forward_weights(): lax.all_gather(w_key, ('dp', 'ctx'), axis=0, tiled=True)  42.1 us
    all_gather x1, other arithmetic, forward_weights(): lax.all_gather(w_out, ('dp', 'ctx'), axis=0, tiled=True)  39.9 us
    all_gather x1, other arithmetic, forward_weights(): lax.all_gather(w_query, ('dp', 'ctx'), axis=0, tiled=True)  39.5 us
  transfers between devices with their start and end apart: 19, of which 8 were waited for; matrix products, arithmetic and copies ran while one was open for 43% of the time, Pallas kernels for 0%

profile of v1, /device:TPU:0, one launch (start us, length us, event | category | flops | bytes accessed | tf_op | source)
XLA Modules:
  0.0 971.4 jit_solution(5822365467697926759)
XLA Ops:
  13.2 47.4 %all-gather.4 = bf16[32,1,9600]{2,1,0:T(2,128)(2,1)S(1)} all-gather(bf16[1,1,9600]{2,1,0:T(2,128)(2,1)S(1)} %reshape.1655), channel_id=1, replica_groups=mesh['dp'=8,'ctx'=4] {'dp','ctx'}, dimensions={0}, use_global_device_ids=true | all-gather | bytes 633600 | tf_op jit(solution)/shard_map/all_gather | solution.py:188
  66.2 42.1 %all-gather.5 = bf16[32,1,9600]{2,1,0:T(2,128)(2,1)S(1)} all-gather(bf16[1,1,9600]{2,1,0:T(2,128)(2,1)S(1)} %reshape.1657), channel_id=1, replica_groups=mesh['dp'=8,'ctx'=4] {'dp','ctx'}, dimensions={0}, use_global_device_ids=true | all-gather | bytes 633600 | tf_op jit(solution)/shard_map/all_gather | solution.py:187
  118.4 8.5 all-gather.2
  128.1 9.6 all-gather.3
  137.8 5.1 all_gather.32
  142.8 5.1 all_gather.76
  147.9 8.4 all-gather
  156.5 8.2 all-gather.1
  166.1 39.5 %reduce.19 = bf16[32,28800]{1,0:T(8,128)(2,1)S(1)} reduce(bf16[32,1,28800]{2,1,0:T(2,128)(2,1)} %all-gather.20.cloned.1.call-done, bf16[]{:T(256)} %constant.92), dimensions={1}, to_apply=%all-gather.6.reduce_sub_computation | reduce | bytes 3686402 | tf_op jit(solution)/shard_map/all_gather | solution.py:186
  211.4 6.8 fusion.152
  218.3 7.7 fusion.6
  226.0 39.9 %reduce.20 = bf16[32,28800]{1,0:T(8,128)(2,1)S(1)} reduce(bf16[32,1,28800]{2,1,0:T(2,128)(2,1)} %all-gather.22.cloned.1.call-done, bf16[]{:T(256)} %constant.92), dimensions={1}, to_apply=%all-gather.7.reduce_sub_computation | reduce | bytes 3686402 | tf_op jit(solution)/shard_map/all_gather | solution.py:189
  268.7 7.2 fusion.44
  279.1 6.9 fusion.151
  286.1 7.8 fusion.7
  293.8 7.0 fusion.47
  303.1 10.0 %reshape.1572 = bf16[960,2560]{1,0:T(8,128)(2,1)} reshape(bf16[2457600]{0:T(1024)(128)(2,1)} %all-gather.14.cloned.1.call-done) | data formatting | bytes 9830400 | tf_op jit(solution)/shard_map/reshape | solution.py:194
  313.1 10.0 %reshape.1573 = bf16[960,2560]{1,0:T(8,128)(2,1)} reshape(bf16[2457600]{0:T(1024)(128)(2,1)} %all-gather.16.cloned.1.call-done) | data formatting | bytes 9830400 | tf_op jit(solution)/shard_map/reshape | solution.py:194
  323.1 5.6 fusion.153
  331.7 11.4 %all-gather.18.cloned.1.call-done = bf16[2457600]{0:T(1024)(128)(2,1)} async-done(((bf16[76800]{0:T(1024)(128)(2,1)}), bf16[2457600]{0:T(1024)(128)(2,1)}) %all-gather.18.cloned.1.call-update) | async-done | bytes 4915216 | tf_op jit(solution)/shard_map/all_gather | solution.py:192
  343.1 9.6 reshape.1574
  352.7 8.9 multiply_convert_fusion.2
  361.6 4.8 fusion.157
  372.9 4.1 multiply_convert_fusion
  385.8 8.4 fusion
  394.1 8.1 fusion.17
  410.8 13.0 %fusion.3 = (f32[5,3,256]{2,1,0:T(4,128)S(1)}, f32[5,1024,256,3]{2,1,3,0:T(8,128)}) fusion(f32[1,5,3,256,1024]{3,4,2,1,0:T(8,128)} %get-tuple-element.86, f32[5,3,256]{2,1,0:T(4,128)S(1)} %log_add_fusion.1, bf16[1024,5,64,1]{0,2,3,1:T(8,128)(2,1)} %bitcast.436, bf16[256,5,3,64]{0,3,2,1:T(8,128)(2,1)S(1)} %bitcast.425), kind=kOutput, calls=%fused_computation.10 | convolution fusion | flops 515109120 | bytes 32634880 | tf_op jit(solution)/shard_map/sckgd,slkd->skgcl/dot_general | solution.py:309
  426.8 7.6 fusion.16
  442.5 5.3 convert_element_type.487
  450.7 4.4 all-to-all-start
  459.3 6.7 fusion.32
  466.1 4.6 add_convert_fusion.3
  470.7 5.3 convert_element_type.493
  479.1 5.1 fusion.159
  484.2 8.9 fusion.37
  493.5 9.0 fusion.34
  502.5 7.6 add_convert_fusion.2
  510.1 8.1 convert_element_type.495
  518.2 6.1 copy.61
  524.3 6.6 fusion.160
  533.0 4.4 all-to-all-start.3
  540.6 23.4 %all-to-all-done.3 = bf16[8,4,28800]{2,0,1:T(8,128)(2,1)} async-done(((bf16[8,4,28800]{2,0,1:T(8,128)(2,1)}), bf16[8,4,28800]{2,0,1:T(8,128)(2,1)}, u32[]{:S(2)}, u32[]{:S(2)}) %all-to-all-start.3) | async-done | bytes 1843232 | tf_op jit(solution)/shard_map/all_to_all | solution.py:111
  564.0 4.2 all-to-all-start.1
  581.9 7.8 add_convert_fusion.1
  589.8 8.1 convert_element_type.497
  597.9 5.0 all-to-all-start.4
  602.9 13.4 %constant_dynamic-slice_fusion.3 = (bf16[8,1,1,76800]{3,1,0,2:T(2,128)(2,1)S(1)}, bf16[8,1,1,76800]{3,1,0,2:T(2,128)(2,1)S(1)}, bf16[8,1,1,76800]{3,1,0,2:T(2,128)(2,1)S(1)}, bf16[8,1,1,76800]{3,1,0,2:T(2,128)(2,1)S(1)}) fusion(bf16[8,4,1,76800]{3,1,0,2:T(4,128)(2,1)} %convert_element_type.497, s32[]{:T(128)S(6)} %select_n.33, s32[]{:T(128)S(6)} %select_n.35, ...), kind=kLoop, calls=%fused_computation.229 | loop fusion | bytes 9830416 | tf_op jit(solution)/shard_map/dynamic-slice
  628.4 7.9 copy.66
  636.2 9.9 %convert_element_type.499 = bf16[8,4,76800]{2,1,0:T(4,128)(2,1)} reshape(bf16[2560,960]{1,0:T(8,128)(2,1)} %copy.66) | data formatting | bytes 9830400 | tf_op jit(solution)/shard_map/convert_element_type | solution.py:119
  646.2 6.1 copy.67
  652.2 7.1 all-to-all-done.4
  659.3 5.0 all-to-all-start.5
  664.4 20.3 %collective-permute-done.2 = bf16[8,1,76800]{2,0,1:T(8,128)(2,1)} collective-permute-done((bf16[8,1,76800]{2,0,1:T(8,128)(2,1)}, bf16[8,1,76800]{2,0,1:T(8,128)(2,1)}, u32[]{:S(2)}, u32[]{:S(2)}) %collective-permute-start.2) | collective-permute-done | bytes 1228832 | tf_op jit(solution)/shard_map/ppermute | solution.py:34
  684.7 27.3 %collective-permute-done.1 = bf16[8,1,76800]{2,0,1:T(8,128)(2,1)} collective-permute-done((bf16[8,1,76800]{2,0,1:T(8,128)(2,1)}, bf16[8,1,76800]{2,0,1:T(8,128)(2,1)}, u32[]{:S(2)}, u32[]{:S(2)}) %collective-permute-start.1) | collective-permute-done | bytes 1228832 | tf_op jit(solution)/shard_map/ppermute | solution.py:34
  712.0 5.2 maximum_bitcast_fusion
  717.2 5.5 gather_fusion
  722.7 4.5 reduce.15
  735.2 4.5 reduce_sum.248
  739.7 24.5 %all-to-all-done.5 = bf16[8,4,76800]{2,0,1:T(8,128)(2,1)} async-done(((bf16[8,4,76800]{2,0,1:T(8,128)(2,1)}), bf16[8,4,76800]{2,0,1:T(8,128)(2,1)}, u32[]{:S(2)}, u32[]{:S(2)}) %all-to-all-start.5) | async-done | bytes 4915232 | tf_op jit(solution)/shard_map/all_to_all | solution.py:118
  764.2 4.5 reduce_sum.250
  770.0 5.2 fusion.58
  775.2 4.8 fusion.59
  787.4 44.7 %all-reduce.7 = (f32[960]{0:T(1024)}, f32[960]{0:T(1024)}) all-reduce(f32[960]{0:T(1024)S(1)} %add.358, f32[960]{0:T(1024)S(1)} %add.363), channel_id=1, replica_groups=mesh['dp'=8,'ctx'=4] {'dp','ctx'}, use_global_device_ids=true, to_apply=%region_20.21 | all-reduce | flops 1920 | bytes 15360 | tf_op jit(solution)/shard_map/psum | solution.py:372
  835.8 110.0 %all-reduce.11.cloned.1.call-done = (bf16[8,28800]{1,0:T(8,128)(2,1)}, bf16[8,9600]{1,0:T(8,128)(2,1)}, bf16[8,9600]{1,0:T(8,128)(2,1)}, bf16[8,28800]{1,0:T(8,1...) async-done(((bf16[8,28800]{1,0:T(8,128)(2,1)}, bf16[8,9600]{1,0:T(8,128)(2,1)}, bf16[8,9600]{1,0:T(8,128)(2,1)}, ...) | async-done | bytes 4915216
  (367 shorter events, 155.5 us)
Async XLA Ops:
  7.2 58.8 %copy-start.2 = (bf16[2,256,960]{1,2,0:T(8,128)(2,1)S(1)}, bf16[2,256,960]{1,2,0:T(8,128)(2,1)}, u32[]{:S(2)}) copy-start(bf16[2,256,960]{1,2,0:T(8,128)(2,1)} %param.13) | copy-start | bytes 2949124
  7.2 59.0 %copy-start.82 = (bf16[9600]{0:T(1024)(128)(2,1)S(1)}, bf16[9600]{0:T(1024)(128)(2,1)}, u32[]{:S(2)}) copy-start(bf16[9600]{0:T(1024)(128)(2,1)} %param.18) | copy-start | bytes 57604
  7.2 158.9 %all-gather.20.cloned.1.call-start = ((), (), s32[]{:S(2)}) async-start(), calls=%async_computation.17 | async-start | bytes 3801600 | tf_op jit(solution)/shard_map/all_gather | solution.py:186
  8.9 217.1 %all-gather.22.cloned.1.call-start = ((), (), s32[]{:S(2)}) async-start(), calls=%async_computation.18 | async-start | bytes 3801600 | tf_op jit(solution)/shard_map/all_gather | solution.py:189
  10.5 292.6 %all-gather.14.cloned.1.call-start = ((), (), s32[]{:S(2)}) async-start(), calls=%async_computation.10 | async-start | bytes 5068800 | tf_op jit(solution)/shard_map/all_gather | solution.py:190
  11.2 301.9 %all-gather.16.cloned.1.call-start = ((), (), s32[]{:S(2)}) async-start(), calls=%async_computation.11 | async-start | bytes 5068800 | tf_op jit(solution)/shard_map/all_gather | solution.py:191
  11.8 331.3 %all-gather.18.cloned.1.call-start = ((), (), s32[]{:S(2)}) async-start(), calls=%async_computation.12 | async-start | bytes 5068800 | tf_op jit(solution)/shard_map/all_gather | solution.py:192
  12.4 518.5 %reduce-scatter.9.cloned.1.call-start = ((), (), s32[]{:S(2)}) async-start(), calls=%async_computation.15 | async-start | bytes 819200 | tf_op jit(solution)/shard_map/reduce_scatter | solution.py:333
  60.6 52.9 %copy-start.72 = (f32[960]{0:T(1024)S(1)}, f32[960]{0:T(1024)}, u32[]{:S(2)}) copy-start(f32[960]{0:T(1024)} %param.16) | copy-start | bytes 11524
  112.8 4.9 copy-start.16
  113.5 94.8 %copy-start.77 = (f32[256]{0:T(256)}, f32[256]{0:T(256)S(1)}, u32[]{:S(2)}) copy-start(f32[256]{0:T(256)S(1)} %get-tuple-element.98) | copy-start | bytes 3076
  115.2 11.6 %copy-start.87 = (s32[2,256]{1,0:T(2,128)S(1)}, s32[2,256]{1,0:T(2,128)}, u32[]{:S(2)}) copy-start(s32[2,256]{1,0:T(2,128)} %param.15) | copy-start | bytes 6148
  115.9 21.9 %copy-start.88 = (s32[2,256]{1,0:T(2,128)S(1)}, s32[2,256]{1,0:T(2,128)}, u32[]{:S(2)}) copy-start(s32[2,256]{1,0:T(2,128)} %param.14) | copy-start | bytes 6148
  117.1 30.8 %copy-start.75 = (bf16[256,320]{0,1:T(8,128)(2,1)S(1)}, bf16[256,320]{0,1:T(8,128)(2,1)}, u32[]{:S(2)}) copy-start(bf16[256,320]{0,1:T(8,128)(2,1)} %convolution_convert_fusion.3) | copy-start | bytes 491524
  127.5 28.9 %copy-start.49 = (f32[256,64]{0,1:T(8,128)}, f32[256,64]{0,1:T(8,128)S(1)}, u32[]{:S(2)}) copy-start(f32[256,64]{0,1:T(8,128)S(1)} %get-tuple-element.62) | copy-start | bytes 196612
  127.5 28.9 %copy-start.52 = (f32[256,64]{0,1:T(8,128)}, f32[256,64]{0,1:T(8,128)S(1)}, u32[]{:S(2)}) copy-start(f32[256,64]{0,1:T(8,128)S(1)} %get-tuple-element.101) | copy-start | bytes 196612
  127.5 83.7 %copy-start.45 = (f32[256,64]{0,1:T(8,128)}, f32[256,64]{0,1:T(8,128)S(1)}, u32[]{:S(2)}) copy-start(f32[256,64]{0,1:T(8,128)S(1)} %get-tuple-element.63) | copy-start | bytes 196612
  164.7 46.7 %copy-start.12 = (bf16[1024,320]{0,1:T(8,128)(2,1)}, bf16[1024,320]{0,1:T(8,128)(2,1)S(1)}, u32[]{:S(2)}) copy-start(bf16[1024,320]{0,1:T(8,128)(2,1)S(1)} %all-gather.1) | copy-start | bytes 1966084
  211.4 6.9 copy-start.18
  226.0 42.7 %copy-start.23 = (bf16[1024,320]{0,1:T(8,128)(2,1)S(1)}, bf16[1024,320]{0,1:T(8,128)(2,1)}, u32[]{:S(2)}) copy-start(bf16[1024,320]{0,1:T(8,128)(2,1)} %all-gather) | copy-start | bytes 1966084
  268.7 7.3 copy-start.3
  276.9 25.9 %copy-start.9 = (f32[256,960]{0,1:T(8,128)}, f32[256,960]{0,1:T(8,128)S(1)}, u32[]{:S(2)}) copy-start(f32[256,960]{0,1:T(8,128)S(1)} %get-tuple-element.88) | copy-start | bytes 2949124
  279.1 7.0 copy-start.19
  286.1 7.8 copy-start.22
  323.1 5.6 copy-start
  331.7 21.0 %copy-start.24 = (bf16[2,256,960]{1,2,0:T(8,128)(2,1)S(1)}, bf16[2,256,960]{1,2,0:T(8,128)(2,1)}, u32[]{:S(2)}) copy-start(bf16[2,256,960]{1,2,0:T(8,128)(2,1)} %param.25) | copy-start | bytes 2949124
  343.1 23.4 %slice-start.8 = ((s8[4915200]{0:T(1024)(128)(4,1)}), s8[720896]{0:T(1024)(128)(4,1)S(1)}, s32[]{:S(2)}) async-start(s8[4915200]{0:T(1024)(128)(4,1)} %bitcast.419), calls=%async_computation.28 | async-start | bytes 1441792
  352.7 13.8 %slice-start.9 = ((s8[4915200]{0:T(1024)(128)(4,1)}), s8[4194304]{0:T(1024)(128)(4,1)S(1)}, s32[]{:S(2)}) async-start(s8[4915200]{0:T(1024)(128)(4,1)} %bitcast.419), calls=%async_computation.29 | async-start | bytes 8388608
  361.6 4.9 copy-start.10
  361.6 4.9 copy-start.29
  361.6 8.1 slice-start.10
  377.0 8.0 slice-start.4
  379.1 5.9 slice-start.5
  379.1 5.9 slice-start.6
  394.1 8.2 copy-start.15
  410.8 13.1 %slice-start = ((s8[15728640]{0:T(1024)(128)(4,1)}), s8[4194304]{0:T(1024)(128)(4,1)S(1)}, s32[]{:S(2)}) async-start(s8[15728640]{0:T(1024)(128)(4,1)} %bitcast.415), calls=%async_computation.20 | async-start | bytes 8388608
  410.8 13.8 %slice-start.1 = ((s8[15728640]{0:T(1024)(128)(4,1)}), s8[4194304]{0:T(1024)(128)(4,1)S(1)}, s32[]{:S(2)}) async-start(s8[15728640]{0:T(1024)(128)(4,1)} %bitcast.415), calls=%async_computation.21 | async-start | bytes 8388608
  410.8 15.2 %slice-start.2 = ((s8[15728640]{0:T(1024)(128)(4,1)}), s8[4194304]{0:T(1024)(128)(4,1)S(1)}, s32[]{:S(2)}) async-start(s8[15728640]{0:T(1024)(128)(4,1)} %bitcast.415), calls=%async_computation.22 | async-start | bytes 8388608
  410.8 16.0 %slice-start.3 = ((s8[15728640]{0:T(1024)(128)(4,1)}), s8[3145728]{0:T(1024)(128)(4,1)S(1)}, s32[]{:S(2)}) async-start(s8[15728640]{0:T(1024)(128)(4,1)} %bitcast.415), calls=%async_computation.23 | async-start | bytes 6291456
  426.8 7.6 copy-start.13
  450.7 82.3 %all-to-all-start = ((bf16[8,4,28800]{2,0,1:T(8,128)(2,1)}), bf16[8,4,28800]{2,0,1:T(8,128)(2,1)}, u32[]{:S(2)}, u32[]{:S(2)}) async-start(bf16[8,4,28800]{2,0,1:T(8,128)(2,1)} %copy.55), calls=%async_computation.4 | async-start | bytes 3686400 | tf_op jit(solution)/shard_map/all_to_all | solution.py:102
  455.1 76.8 %reduce-scatter.5.cloned.1.call-start = ((), (), s32[]{:S(2)}) async-start(), calls=%async_computation.13 | async-start | bytes 819200 | tf_op jit(solution)/shard_map/reduce_scatter | solution.py:333
  466.1 102.1 %reduce-scatter.7.cloned.1.call-start = ((), (), s32[]{:S(2)}) async-start(), calls=%async_computation.14 | async-start | bytes 819200 | tf_op jit(solution)/shard_map/reduce_scatter | solution.py:339
  493.2 77.4 %reduce-scatter.11.cloned.1.call-start = ((), (), s32[]{:S(2)}) async-start(), calls=%async_computation.16 | async-start | bytes 819200 | tf_op jit(solution)/shard_map/reduce_scatter | solution.py:339
  493.5 9.1 copy-start.62
  530.9 6.6 copy-start.68
  532.0 5.6 copy-start.69
  533.0 31.0 %all-to-all-start.3 = ((bf16[8,4,28800]{2,0,1:T(8,128)(2,1)}), bf16[8,4,28800]{2,0,1:T(8,128)(2,1)}, u32[]{:S(2)}, u32[]{:S(2)}) async-start(bf16[8,4,28800]{2,0,1:T(8,128)(2,1)} %copy.60), calls=%async_computation.7 | async-start | bytes 3686400 | tf_op jit(solution)/shard_map/all_to_all | solution.py:111
  564.0 14.1 %all-to-all-start.1 = ((bf16[8,4,9600]{2,0,1:T(8,128)(2,1)}), bf16[8,4,9600]{2,0,1:T(8,128)(2,1)}, u32[]{:S(2)}, u32[]{:S(2)}) async-start(bf16[8,4,9600]{2,0,1:T(8,128)(2,1)} %copy.57), calls=%async_computation.5 | async-start | bytes 1228800 | tf_op jit(solution)/shard_map/all_to_all | solution.py:105
  578.1 19.9 %all-to-all-start.2 = ((bf16[8,4,9600]{2,0,1:T(8,128)(2,1)}), bf16[8,4,9600]{2,0,1:T(8,128)(2,1)S(1)}, u32[]{:S(2)}, u32[]{:S(2)}) async-start(bf16[8,4,9600]{2,0,1:T(8,128)(2,1)} %copy.59), calls=%async_computation.6 | async-start | bytes 1228800 | tf_op jit(solution)/shard_map/all_to_all | solution.py:108
  597.9 61.4 %all-to-all-start.4 = ((bf16[8,4,76800]{2,0,1:T(8,128)(2,1)}), bf16[8,4,76800]{2,0,1:T(8,128)(2,1)}, u32[]{:S(2)}, u32[]{:S(2)}) async-start(bf16[8,4,76800]{2,0,1:T(8,128)(2,1)} %copy.61), calls=%async_computation.8 | async-start | bytes 9830400 | tf_op jit(solution)/shard_map/all_to_all | solution.py:114
  617.7 5.1 copy-start.89
  617.7 67.0 %collective-permute-start.2 = (bf16[8,1,76800]{2,0,1:T(8,128)(2,1)}, bf16[8,1,76800]{2,0,1:T(8,128)(2,1)}, u32[]{:S(2)}, u32[]{:S(2)}) collective-permute-start(bf16[8,1,76800]{2,0,1:T(8,128)(2,1)} %bitcast.411), channel_id=1, source_target_pairs={{0,3},{1,2},{2,1},{3,0},{4,7},{5,6},{6,5},{7,4},{8,11},{9,10},{10,... | collective-permute-start | bytes 3686408 | tf_op jit(solution)/shard_map/ppermute | solution.py:34
  621.0 91.0 %collective-permute-start.1 = (bf16[8,1,76800]{2,0,1:T(8,128)(2,1)}, bf16[8,1,76800]{2,0,1:T(8,128)(2,1)}, u32[]{:S(2)}, u32[]{:S(2)}) collective-permute-start(bf16[8,1,76800]{2,0,1:T(8,128)(2,1)} %bitcast.412), channel_id=1, source_target_pairs={{0,2},{1,3},{2,0},{3,1},{4,6},{5,7},{6,4},{7,5},{8,10},{9,11},{10,... | collective-permute-start | bytes 3686408 | tf_op jit(solution)/shard_map/ppermute | solution.py:34
  622.8 89.2 %collective-permute-start = (bf16[8,1,76800]{2,0,1:T(8,128)(2,1)}, bf16[8,1,76800]{2,0,1:T(8,128)(2,1)}, u32[]{:S(2)}, u32[]{:S(2)}) collective-permute-start(bf16[8,1,76800]{2,0,1:T(8,128)(2,1)} %bitcast.413), channel_id=1, source_target_pairs={{0,1},{1,0},{2,3},{3,2},{4,5},{5,4},{6,7},{7,6},{8,9},{9,8},{10,11... | collective-permute-start | bytes 3686408 | tf_op jit(solution)/shard_map/ppermute | solution.py:34
  659.3 104.9 %all-to-all-start.5 = ((bf16[8,4,76800]{2,0,1:T(8,128)(2,1)}), bf16[8,4,76800]{2,0,1:T(8,128)(2,1)}, u32[]{:S(2)}, u32[]{:S(2)}) async-start(bf16[8,4,76800]{2,0,1:T(8,128)(2,1)} %copy.67), calls=%async_computation.9 | async-start | bytes 9830400 | tf_op jit(solution)/shard_map/all_to_all | solution.py:118
  664.3 281.5 %all-reduce.11.cloned.1.call-start = ((), (), s32[]{:S(2)}) async-start(), calls=%async_computation.19 | async-start | bytes 9830400
  770.0 5.2 copy-start.11
  770.0 5.2 copy-start.64
  775.2 5.9 copy-start.40
  775.2 5.9 copy-start.44
  784.1 47.9 %copy-start.6 = (f32[256,960]{0,1:T(8,128)S(1)}, f32[256,960]{0,1:T(8,128)}, u32[]{:S(2)}) copy-start(f32[256,960]{0,1:T(8,128)} %copy-done.5) | copy-start | bytes 2949124
  784.1 47.9 %copy-start.84 = (f32[256]{0:T(256)S(1)}, f32[256]{0:T(256)}, u32[]{:S(2)}) copy-start(f32[256]{0:T(256)} %get-tuple-element.73) | copy-start | bytes 3076
  784.1 47.9 %copy-start.85 = (f32[256]{0:T(256)S(1)}, f32[256]{0:T(256)}, u32[]{:S(2)}) copy-start(f32[256]{0:T(256)} %get-tuple-element.99) | copy-start | bytes 3076
  (60 other events, 126.0 us)
Sparse Core Ops, SparseCore 0:
  11.5 66.6 all-gather.19
  81.7 61.2 all-gather.21
  145.8 65.4 all-gather.13
  214.0 63.1 all-gather.15
  279.9 63.1 all-gather.17
  408.4 21.2 reduce-scatter.8
  466.2 22.5 reduce-scatter.4
  493.3 22.5 reduce-scatter.6
  524.5 26.0 reduce-scatter.10
  768.9 176.8 all-reduce.10
